TPU v7x, 256 devices: a whole 4x4x8 slice. The times are simulated.
256 devices in a mesh: grid: 16 (over y, x), day: 16 (over z, core).
Axes of the slice: x: 4, y: 4, z: 8, core: 2. Of those that a mesh axis runs over, the one named last changes fastest.
Arguments:
- anomalies: bfloat16 [16384, 65536], P('day', 'grid'), may hold values from -6 to 6
- eofs: bfloat16 [64, 65536], P(None, ('grid', 'day')), may hold values from -0.0234375 to 0.0234375
- means_init: float32 [8, 64], replicated, may hold values from -4 to 4
- variances: float32 [8, 64], replicated, may hold values from 0.05 to 2
- mixing: float32 [8], replicated, may hold values from 0.5 to 2
Outputs:
- regime_means: float32 [8, 64], replicated
- regime_covs: float32 [8, 64, 64], replicated
- regime_weights: float32 [8], replicated
- membership: float32 [8, 16384], P(None, 'day')
- composites: bfloat16 [8, 65536], P(None, ('grid', 'day'))
All inputs are finite; a program needn't handle non-finite values.
Results may differ from a plain program's by a relative error of at most 0.0034.
Values may be sent and summed in bfloat16 or wider, within the bound.
No kernel may reach another device: no remote copies, remote signals or barrier semaphores. Data moves between devices by JAX's collectives and lax.ppermute only.
A program may use at most 64 MiB of HBM per device.

v0:
```python
import jax
import jax.numpy as jnp
from jax import lax
from jax.sharding import PartitionSpec as P

ITERS = 2
PRECISE = lax.Precision.HIGHEST
REG = 0.01


def log_density(pcs_t, means, covs, weights):
    regimes = means.shape[0]
    width = means.shape[1]
    eye = jnp.broadcast_to(jnp.eye(width, dtype=jnp.float32), (regimes, width, width))
    factor = jnp.linalg.cholesky(covs)
    inverse = lax.linalg.triangular_solve(factor, eye, left_side=True, lower=True)
    centred = pcs_t[None, :, :] - means[:, :, None]
    shifted = jnp.einsum("rkj,rjd->rkd", inverse, centred, precision=PRECISE)
    logdet = jnp.sum(jnp.log(jnp.diagonal(factor, axis1=1, axis2=2)), axis=1)
    return jnp.log(weights)[:, None] - logdet[:, None] - 0.5 * jnp.sum(shifted * shifted, axis=1)


def responsibilities(pcs_t, means, covs, weights):
    logp = log_density(pcs_t, means, covs, weights)
    top = jnp.max(logp, axis=0, keepdims=True)
    expo = jnp.exp(logp - top)
    return expo / jnp.sum(expo, axis=0, keepdims=True)


def second_moments(pcs_t, resp, means):
    diff = pcs_t[None, :, :] - means[:, :, None]
    return jnp.einsum("rkd,rjd->rkj", diff * resp[:, None, :], diff, precision=PRECISE)


def total_days(values):
    return lax.psum(values, "day")


def first_moments(pcs_t, resp):
    return lax.dot_general(resp, pcs_t, (((1,), (1,)), ((), ())), precision=PRECISE)


def update(pcs_t, resp, eye):
    counts, sums = total_days((jnp.sum(resp, axis=1), first_moments(pcs_t, resp)))
    counted = jnp.maximum(counts, 1.0)
    means = sums / counted[:, None]
    second = total_days(second_moments(pcs_t, resp, means))
    covs = second / counted[:, None, None] + REG * eye[None]
    weights = counted / jnp.sum(counted)
    return (means, covs, weights)


def body(anomalies, eofs, means_init, variances, mixing):
    width = eofs.shape[0]
    partial_pcs = lax.dot_general(
        anomalies,
        lax.all_gather(eofs, "day", axis=1, tiled=True),
        (((1,), (1,)), ((), ())),
        preferred_element_type=jnp.float32,
    )
    pcs = lax.psum(partial_pcs, "grid")
    pcs_t = pcs.T
    eye = jnp.eye(width, dtype=jnp.float32)
    means = means_init
    covs = variances[:, :, None] * eye[None]
    weights = mixing / jnp.sum(mixing)
    for step in range(ITERS):
        resp = responsibilities(pcs_t, means, covs, weights)
        means, covs, weights = update(pcs_t, resp, eye)
    member = responsibilities(pcs_t, means, covs, weights)
    counts = lax.psum(jnp.sum(member, axis=1), "day")
    counted = jnp.maximum(counts, 1.0)
    terms = jnp.dot(member.astype(jnp.bfloat16), anomalies, preferred_element_type=jnp.float32)
    sums = lax.psum_scatter(terms, "day", scatter_dimension=1, tiled=True)
    composites = (sums / counted[:, None]).astype(jnp.bfloat16)
    return (means, covs, weights, member, composites)


def solution(mesh):
    in_specs = (P("day", "grid"), P(None, ("grid", "day")), P(), P(), P())
    out_specs = (P(), P(), P(), P(None, "day"), P(None, ("grid", "day")))
    return jax.shard_map(body, mesh=mesh, in_specs=in_specs, out_specs=out_specs, check_vma=False)
```

profile of v0, /device:TPU:2, one launch (start us, length us, event | category | flops | bytes accessed | tf_op | source)
XLA Modules:
  0.0 667.7 jit_solution(10305190547740485479)
XLA Ops:
  7.2 21.7 %all_gather.3 = bf16[64,4096]{1,0:T(8,128)(2,1)S(1)} all-gather(bf16[64,256]{1,0:T(8,128)(2,1)} %param.9), channel_id=1, replica_groups=mesh['grid'=16,'day'=16] {'day'}, dimensions={1}, use_global_device_ids=true | all-gather | bytes 557056 | tf_op jit(solution)/shard_map/all_gather | solution.py:57
  28.9 6.8 %fusion.61 = f32[1024,64]{0,1:T(8,128)} fusion(bf16[1024,4096]{1,0:T(8,128)(2,1)} %param.8, bf16[64,4096]{1,0:T(8,128)(2,1)S(1)} %all_gather.3), kind=kOutput, calls=%fused_computation.101 | convolution fusion | flops 536870912 | bytes 9175040 | tf_op jit(solution)/shard_map/dot_general | solution.py:55
  36.0 46.9 %custom-call.16 = f32[8,64,64]{2,1,0:T(8,128)S(1)} custom-call(f32[8,64,64]{2,1,0:T(8,128)S(1)} %fusion.36), custom_call_target="Cholesky" | custom-call | tf_op jit(solution)/shard_map/jit(cholesky)/cholesky | solution.py:15
  86.0 39.3 %custom-call.17 = f32[8,1,64,64]{2,3,1,0:T(8,128)S(1)} custom-call(f32[8,1,64,64]{3,2,1,0:T(8,128)S(1)} %get-tuple-element.33), custom_call_target="InvertDiagBlocksLowerTriangular" | custom-call | tf_op jit(solution)/shard_map/triangular_solve/custom-call.0 | solution.py:16
  125.9 3.6 all-reduce.6.cloned.1.call-done
  129.6 3.0 multiply_reduce_fusion.2
  132.9 1.2 fusion.62
  134.1 25.0 %all-reduce.1 = (f32[8,64]{1,0:T(8,128)S(1)}, f32[8]{0:T(128)S(1)}) all-reduce(f32[8,64]{1,0:T(8,128)S(1)} %fusion.62, f32[8]{0:T(128)S(1)} %get-tuple-element.31), channel_id=1, replica_groups=mesh['grid'=16,'day'=16] {'day'}, use_global_device_ids=true, to_apply=%region_11.0 | all-reduce | flops 520 | bytes 4160 | tf_op jit(solution)/shard_map/psum | solution.py:36
  159.8 4.2 fusion.6
  164.2 107.1 %all-reduce.8.cloned.1.call-done = f32[8,64,64]{1,2,0:T(8,128)} async-done(((f32[8,64,64]{1,2,0:T(8,128)}), f32[8,64,64]{1,2,0:T(8,128)}) %all-reduce.8.cloned.1.call-update) | async-done | bytes 131088 | tf_op jit(solution)/shard_map/psum | solution.py:36
  273.6 46.9 %custom-call.18 = f32[8,64,64]{2,1,0:T(8,128)S(1)} custom-call(f32[8,64,64]{2,1,0:T(8,128)S(1)} %fusion.33), custom_call_target="Cholesky" | custom-call | tf_op jit(solution)/shard_map/jit(cholesky)/cholesky | solution.py:15
  320.8 39.3 %custom-call.19 = f32[8,1,64,64]{2,3,1,0:T(8,128)S(1)} custom-call(f32[8,1,64,64]{3,2,1,0:T(8,128)S(1)} %get-tuple-element.29), custom_call_target="InvertDiagBlocksLowerTriangular" | custom-call | tf_op jit(solution)/shard_map/triangular_solve/custom-call.0 | solution.py:16
  360.8 2.0 multiply_reduce_fusion.1
  365.7 26.9 %all-reduce = (f32[8,64]{1,0:T(8,128)S(1)}, f32[8]{0:T(128)S(1)}) all-reduce(f32[8,64]{1,0:T(8,128)S(1)} %fusion.63, f32[8]{0:T(128)S(1)} %get-tuple-element.27), channel_id=1, replica_groups=mesh['grid'=16,'day'=16] {'day'}, use_global_device_ids=true, to_apply=%region_17.0 | all-reduce | flops 520 | bytes 4160 | tf_op jit(solution)/shard_map/psum | solution.py:36
  393.3 3.1 fusion.2
  396.7 106.8 %all-reduce.10.cloned.1.call-done = f32[8,64,64]{1,2,0:T(8,128)} async-done(((f32[8,64,64]{1,2,0:T(8,128)}), f32[8,64,64]{1,2,0:T(8,128)}) %all-reduce.10.cloned.1.call-update) | async-done | bytes 131088 | tf_op jit(solution)/shard_map/psum | solution.py:36
  504.7 1.2 fusion.30
  505.9 46.9 %custom-call.20 = f32[8,64,64]{2,1,0:T(8,128)S(1)} custom-call(f32[8,64,64]{2,1,0:T(8,128)S(1)} %fusion.30), custom_call_target="Cholesky" | custom-call | tf_op jit(solution)/shard_map/jit(cholesky)/cholesky | solution.py:15
  553.0 39.3 %custom-call.21 = f32[8,1,64,64]{2,3,1,0:T(8,128)S(1)} custom-call(f32[8,1,64,64]{3,2,1,0:T(8,128)S(1)} %get-tuple-element.25), custom_call_target="InvertDiagBlocksLowerTriangular" | custom-call | tf_op jit(solution)/shard_map/triangular_solve/custom-call.0 | solution.py:16
  593.0 2.0 multiply_reduce_fusion
  598.1 5.2 fusion.51
  603.4 26.4 %psum.63 = f32[8]{0:T(128)S(1)} all-reduce(f32[8]{0:T(128)S(1)} %get-tuple-element.21), channel_id=1, replica_groups=mesh['grid'=16,'day'=16] {'day'}, use_global_device_ids=true, to_apply=%region_28.31 | all-reduce | flops 8 | bytes 64 | tf_op jit(solution)/shard_map/psum | solution.py:71
  629.8 30.0 %reduce-scatter.2.cloned.1.call-done = f32[8,256]{1,0:T(8,128)} async-done(((f32[8,4096]{1,0:T(8,128)}), f32[8,256]{1,0:T(8,128)}) %reduce-scatter.2.cloned.1.call-update) | async-done | bytes 8208 | tf_op jit(solution)/shard_map/reduce_scatter | solution.py:74
  659.8 1.4 divide_convert_fusion
  (75 shorter events, 17.4 us)
Async XLA Ops:
  7.2 122.4 %all-reduce.6.cloned.1.call-start = ((), (), s32[]{:S(2)}) async-start(), calls=%async_computation.1 | async-start | bytes 524288 | tf_op jit(solution)/shard_map/psum | solution.py:61
  28.9 6.9 %copy-start.3 = (f32[8,64]{1,0:T(8,128)S(1)}, f32[8,64]{1,0:T(8,128)}, u32[]{:S(2)}) copy-start(f32[8,64]{1,0:T(8,128)} %param.11) | copy-start | bytes 6148
  35.7 235.7 %all-reduce.8.cloned.1.call-start = ((), (), s32[]{:S(2)}) async-start(), calls=%async_computation.2 | async-start | bytes 524288 | tf_op jit(solution)/shard_map/psum | solution.py:36
  35.9 48.8 %copy-start.5 = (f32[8]{0:T(128)S(1)}, f32[8]{0:T(128)}, u32[]{:S(2)}) copy-start(f32[8]{0:T(128)} %param.12) | copy-start | bytes 100
  36.0 93.6 %copy-start.6 = (f32[8,64]{1,0:T(8,128)S(1)}, f32[8,64]{1,0:T(8,128)}, u32[]{:S(2)}) copy-start(f32[8,64]{1,0:T(8,128)} %param.10) | copy-start | bytes 6148
  164.0 196.8 %copy-start = (f32[1024,64]{0,1:T(8,128)S(1)}, f32[1024,64]{0,1:T(8,128)}, u32[]{:S(2)}) copy-start(f32[1024,64]{0,1:T(8,128)} %all-reduce.6.cloned.1.call-done) | copy-start | bytes 786436
  164.0 339.5 %all-reduce.10.cloned.1.call-start = ((), (), s32[]{:S(2)}) async-start(), calls=%async_computation.3 | async-start | bytes 524288 | tf_op jit(solution)/shard_map/psum | solution.py:36
  393.3 199.7 %copy-start.4 = (f32[8,64]{1,0:T(8,128)}, f32[8,64]{1,0:T(8,128)S(1)}, u32[]{:S(2)}) copy-start(f32[8,64]{1,0:T(8,128)S(1)} %broadcast_divide_fusion) | copy-start | bytes 6148
  396.4 263.4 %reduce-scatter.2.cloned.1.call-start = ((), (), s32[]{:S(2)}) async-start(), calls=%async_computation.4 | async-start | bytes 139264 | tf_op jit(solution)/shard_map/reduce_scatter | solution.py:74
  504.7 91.0 %copy-start.1 = (f32[8,64,64]{2,1,0:T(8,128)}, f32[8,64,64]{2,1,0:T(8,128)S(1)}, u32[]{:S(2)}) copy-start(f32[8,64,64]{2,1,0:T(8,128)S(1)} %copy.27) | copy-start | bytes 393220
  598.1 5.3 copy-start.2
Sparse Core Ops, SparseCore 0:
  35.8 93.7 all-reduce.5
  164.1 107.2 all-reduce.7
  396.6 106.8 all-reduce.9
  603.5 56.2 reduce-scatter.1
where the time goes:
time: 668 us
  other arithmetic  271 us (41%)
  waiting for transfers between devices  248 us (37%)
  blocking collectives  100 us (15%)
  matrix products  29.6 us (4%)
  between operations  14.1 us (2%)
    psum x2, waiting for transfers between devices, total_days(): return lax.psum(values, 'day')  214 us
    another operation x10, other arithmetic, log_density(): factor = jnp.linalg.cholesky(covs)  141 us
    another operation x6, other arithmetic, log_density(): lax.linalg.triangular_solve(factor, eye, left_side=True, lower=True)  118 us
    psum x2, blocking collectives, total_days(): return lax.psum(values, 'day')  52 us
    reduce_scatter x1, waiting for transfers between devices, body(): sums = lax.psum_scatter(terms, 'day', scatter_dimension=1, tiled=True)  30 us
    psum x1, blocking collectives, body(): counts = lax.psum(jnp.sum(member, axis=1), 'day')  26.4 us
    all_gather x1, blocking collectives, body(): lax.all_gather(eofs, 'day', axis=1, tiled=True)  21.7 us
  transfers between devices with their start and end apart: 4, of which 4 were waited for; matrix products, arithmetic and copies ran while one was open for 13% of the time, Pallas kernels for 0%

commit v1 on v0

--- a/solution.py
+++ b/solution.py
@@ -54,7 +54,9 @@
     width = eofs.shape[0]
     partial_pcs = lax.dot_general(
         anomalies,
-        lax.all_gather(eofs, "day", axis=1, tiled=True),
+        jnp.concatenate(
+            lax.all_to_all(jnp.stack([eofs] * lax.axis_size("day")), "day", 0, 0), axis=1
+        ),
         (((1,), (1,)), ((), ())),
         preferred_element_type=jnp.float32,
     )

time: 668 us -> 710 us (1.063)
  waiting for transfers between devices: 248 us -> 300 us
  blocking collectives: 100 us -> 78.3 us
  starting transfers between devices: 0.57 us -> 9.14 us
    psum x1, waiting for transfers between devices: 3.6 us -> 55.6 us  [body(): pcs = lax.psum(partial_pcs, 'grid')]
    all_gather x1 -> x0, blocking collectives: 21.7 us -> none  [body(): lax.all_gather(eofs, 'day', axis=1, tiled=True)]
    all_to_all x0 -> x1, starting transfers between devices: none -> 8.57 us  [body(): lax.all_to_all(jnp.stack([eofs] * lax.axis_size('day')), 'day', 0, 0)]
  transfers between devices with their start and end apart: 4 -> 5, of which waited for: 4 -> 4; matrix products, arithmetic and copies ran while one was open for 13% -> 13% of each run, Pallas kernels for 0% -> 0%
where the time goes in v1:
time: 710 us; the launch traced here: 709 us
  waiting for transfers between devices  300 us (42%)
  other arithmetic  272 us (38%)
  blocking collectives  78.3 us (11%)
  matrix products  29.6 us (4%)
  between operations  14.1 us (2%)
  starting transfers between devices  9.14 us (1%)
    psum x2, waiting for transfers between devices, total_days(): return lax.psum(values, 'day')  214 us
    another operation x10, other arithmetic, log_density(): factor = jnp.linalg.cholesky(covs)  141 us
    another operation x6, other arithmetic, log_density(): lax.linalg.triangular_solve(factor, eye, left_side=True, lower=True)  118 us
    psum x1, waiting for transfers between devices, body(): pcs = lax.psum(partial_pcs, 'grid')  55.6 us
    psum x2, blocking collectives, total_days(): return lax.psum(values, 'day')  51.9 us
    reduce_scatter x1, waiting for transfers between devices, body(): sums = lax.psum_scatter(terms, 'day', scatter_dimension=1, tiled=True)  30 us
    psum x1, blocking collectives, body(): counts = lax.psum(jnp.sum(member, axis=1), 'day')  26.4 us
  transfers between devices with their start and end apart: 5, of which 4 were waited for; matrix products, arithmetic and copies ran while one was open for 13% of the time, Pallas kernels for 0%

profile of v1, /device:TPU:2, one launch (start us, length us, event | category | flops | bytes accessed | tf_op | source)
XLA Modules:
  0.0 709.0 jit_solution(16098534036309891774)
XLA Ops:
  7.2 1.6 stack.2
  8.8 8.6 %all-to-all-start = ((bf16[16,64,256]{2,1,0:T(8,128)(2,1)}), bf16[16,64,256]{2,1,0:T(8,128)(2,1)S(1)}, u32[]{:S(2)}, u32[]{:S(2)}) async-start(bf16[16,64,256]{2,1,0:T(8,128)(2,1)} %stack.2), calls=%async_computation | async-start | bytes 1048576 | tf_op jit(solution)/shard_map/all_to_all | solution.py:58
  18.3 46.9 %custom-call.16 = f32[8,64,64]{2,1,0:T(8,128)S(1)} custom-call(f32[8,64,64]{2,1,0:T(8,128)S(1)} %fusion.36), custom_call_target="Cholesky" | custom-call | tf_op jit(solution)/shard_map/jit(cholesky)/cholesky | solution.py:15
  67.8 6.7 fusion.61
  75.3 39.3 %custom-call.17 = f32[8,1,64,64]{2,3,1,0:T(8,128)S(1)} custom-call(f32[8,1,64,64]{3,2,1,0:T(8,128)S(1)} %get-tuple-element.43), custom_call_target="InvertDiagBlocksLowerTriangular" | custom-call | tf_op jit(solution)/shard_map/triangular_solve/custom-call.0 | solution.py:16
  115.2 55.6 %all-reduce.6.cloned.1.call-done = f32[1024,64]{0,1:T(8,128)} async-done(((f32[1024,64]{0,1:T(8,128)}), f32[1024,64]{0,1:T(8,128)}) %all-reduce.6.cloned.1.call-update) | async-done | bytes 262160 | tf_op jit(solution)/shard_map/psum | solution.py:63
  170.8 3.0 multiply_reduce_fusion.2
  174.1 1.2 fusion.62
  175.4 25.0 %all-reduce.1 = (f32[8,64]{1,0:T(8,128)S(1)}, f32[8]{0:T(128)S(1)}) all-reduce(f32[8,64]{1,0:T(8,128)S(1)} %fusion.62, f32[8]{0:T(128)S(1)} %get-tuple-element.41), channel_id=1, replica_groups=mesh['grid'=16,'day'=16] {'day'}, use_global_device_ids=true, to_apply=%region_11.0 | all-reduce | flops 520 | bytes 4160 | tf_op jit(solution)/shard_map/psum | solution.py:36
  201.0 4.2 fusion.6
  205.5 107.3 %all-reduce.8.cloned.1.call-done = f32[8,64,64]{1,2,0:T(8,128)} async-done(((f32[8,64,64]{1,2,0:T(8,128)}), f32[8,64,64]{1,2,0:T(8,128)}) %all-reduce.8.cloned.1.call-update) | async-done | bytes 131088 | tf_op jit(solution)/shard_map/psum | solution.py:36
  315.0 46.9 %custom-call.18 = f32[8,64,64]{2,1,0:T(8,128)S(1)} custom-call(f32[8,64,64]{2,1,0:T(8,128)S(1)} %fusion.33), custom_call_target="Cholesky" | custom-call | tf_op jit(solution)/shard_map/jit(cholesky)/cholesky | solution.py:15
  362.2 39.3 %custom-call.19 = f32[8,1,64,64]{2,3,1,0:T(8,128)S(1)} custom-call(f32[8,1,64,64]{3,2,1,0:T(8,128)S(1)} %get-tuple-element.39), custom_call_target="InvertDiagBlocksLowerTriangular" | custom-call | tf_op jit(solution)/shard_map/triangular_solve/custom-call.0 | solution.py:16
  402.2 2.0 multiply_reduce_fusion.1
  407.0 26.9 %all-reduce = (f32[8,64]{1,0:T(8,128)S(1)}, f32[8]{0:T(128)S(1)}) all-reduce(f32[8,64]{1,0:T(8,128)S(1)} %fusion.63, f32[8]{0:T(128)S(1)} %get-tuple-element.37), channel_id=1, replica_groups=mesh['grid'=16,'day'=16] {'day'}, use_global_device_ids=true, to_apply=%region_17.0 | all-reduce | flops 520 | bytes 4160 | tf_op jit(solution)/shard_map/psum | solution.py:36
  434.7 3.1 fusion.2
  438.1 106.6 %all-reduce.10.cloned.1.call-done = f32[8,64,64]{1,2,0:T(8,128)} async-done(((f32[8,64,64]{1,2,0:T(8,128)}), f32[8,64,64]{1,2,0:T(8,128)}) %all-reduce.10.cloned.1.call-update) | async-done | bytes 131088 | tf_op jit(solution)/shard_map/psum | solution.py:36
  547.1 46.9 %custom-call.20 = f32[8,64,64]{2,1,0:T(8,128)S(1)} custom-call(f32[8,64,64]{2,1,0:T(8,128)S(1)} %fusion.30), custom_call_target="Cholesky" | custom-call | tf_op jit(solution)/shard_map/jit(cholesky)/cholesky | solution.py:15
  594.3 39.3 %custom-call.21 = f32[8,1,64,64]{2,3,1,0:T(8,128)S(1)} custom-call(f32[8,1,64,64]{3,2,1,0:T(8,128)S(1)} %get-tuple-element.35), custom_call_target="InvertDiagBlocksLowerTriangular" | custom-call | tf_op jit(solution)/shard_map/triangular_solve/custom-call.0 | solution.py:16
  634.2 2.0 multiply_reduce_fusion
  639.4 5.2 fusion.51
  644.6 26.4 %psum.63 = f32[8]{0:T(128)S(1)} all-reduce(f32[8]{0:T(128)S(1)} %get-tuple-element.31), channel_id=1, replica_groups=mesh['grid'=16,'day'=16] {'day'}, use_global_device_ids=true, to_apply=%region_28.31 | all-reduce | flops 8 | bytes 64 | tf_op jit(solution)/shard_map/psum | solution.py:73
  671.1 30.0 %reduce-scatter.2.cloned.1.call-done = f32[8,256]{1,0:T(8,128)} async-done(((f32[8,4096]{1,0:T(8,128)}), f32[8,256]{1,0:T(8,128)}) %reduce-scatter.2.cloned.1.call-update) | async-done | bytes 8208 | tf_op jit(solution)/shard_map/reduce_scatter | solution.py:76
  701.1 1.4 divide_convert_fusion
  (78 shorter events, 19.3 us)
Async XLA Ops:
  7.2 11.1 %copy-start.3 = (f32[8,64]{1,0:T(8,128)S(1)}, f32[8,64]{1,0:T(8,128)}, u32[]{:S(2)}) copy-start(f32[8,64]{1,0:T(8,128)} %param.11) | copy-start | bytes 6148
  8.8 58.9 %all-to-all-start = ((bf16[16,64,256]{2,1,0:T(8,128)(2,1)}), bf16[16,64,256]{2,1,0:T(8,128)(2,1)S(1)}, u32[]{:S(2)}, u32[]{:S(2)}) async-start(bf16[16,64,256]{2,1,0:T(8,128)(2,1)} %stack.2), calls=%async_computation | async-start | bytes 1048576 | tf_op jit(solution)/shard_map/all_to_all | solution.py:58
  17.4 153.4 %all-reduce.6.cloned.1.call-start = ((), (), s32[]{:S(2)}) async-start(), calls=%async_computation.2 | async-start | bytes 524288 | tf_op jit(solution)/shard_map/psum | solution.py:63
  18.3 47.9 %copy-start.5 = (f32[8]{0:T(128)S(1)}, f32[8]{0:T(128)}, u32[]{:S(2)}) copy-start(f32[8]{0:T(128)} %param.12) | copy-start | bytes 100
  67.8 103.0 %copy-start.6 = (f32[8,64]{1,0:T(8,128)S(1)}, f32[8,64]{1,0:T(8,128)}, u32[]{:S(2)}) copy-start(f32[8,64]{1,0:T(8,128)} %param.10) | copy-start | bytes 6148
  74.5 238.2 %all-reduce.8.cloned.1.call-start = ((), (), s32[]{:S(2)}) async-start(), calls=%async_computation.3 | async-start | bytes 524288 | tf_op jit(solution)/shard_map/psum | solution.py:36
  205.2 197.0 %copy-start = (f32[1024,64]{0,1:T(8,128)S(1)}, f32[1024,64]{0,1:T(8,128)}, u32[]{:S(2)}) copy-start(f32[1024,64]{0,1:T(8,128)} %all-reduce.6.cloned.1.call-done) | copy-start | bytes 786436
  205.2 339.5 %all-reduce.10.cloned.1.call-start = ((), (), s32[]{:S(2)}) async-start(), calls=%async_computation.4 | async-start | bytes 524288 | tf_op jit(solution)/shard_map/psum | solution.py:36
  434.7 199.6 %copy-start.4 = (f32[8,64]{1,0:T(8,128)}, f32[8,64]{1,0:T(8,128)S(1)}, u32[]{:S(2)}) copy-start(f32[8,64]{1,0:T(8,128)S(1)} %broadcast_divide_fusion) | copy-start | bytes 6148
  437.8 263.2 %reduce-scatter.2.cloned.1.call-start = ((), (), s32[]{:S(2)}) async-start(), calls=%async_computation.5 | async-start | bytes 139264 | tf_op jit(solution)/shard_map/reduce_scatter | solution.py:76
  545.9 91.0 %copy-start.1 = (f32[8,64,64]{2,1,0:T(8,128)}, f32[8,64,64]{2,1,0:T(8,128)S(1)}, u32[]{:S(2)}) copy-start(f32[8,64,64]{2,1,0:T(8,128)S(1)} %copy.59) | copy-start | bytes 393220
  639.4 5.3 copy-start.2
Sparse Core Ops, SparseCore 0:
  74.7 96.0 all-reduce.5
  205.3 107.3 all-reduce.7
  437.9 106.7 all-reduce.9
  644.8 56.2 reduce-scatter.1
